TPU v7x, 32 devices: a whole 2x2x4 slice. The times are simulated.
32 devices in a mesh: dp: 8 (over y, x, core), tensor: 4 (over z).
Axes of the slice: x: 2, y: 2, z: 4, core: 2. Of those that a mesh axis runs over, the one named last changes fastest.
Arguments:
- tokens: bfloat16 [5120, 2048], P('dp'), may hold values from -6 to 6
- cotangent: bfloat16 [5120, 2048], P('dp'), may hold values from -6 to 6
- token_slots: int32 [5120], replicated, may hold values from 0 to 8191, as said below
- lengths: int32 [8, 3], P('dp'), may hold values from 0 to 1024, as said below
- mixer_gain: bfloat16 [2048], replicated, may hold values from 0.5 to 1.5
- query_weight: bfloat16 [2048, 1024], P(None, 'tensor'), may hold values from -0.125 to 0.125
- key_weight: bfloat16 [2048, 1024], P(None, 'tensor'), may hold values from -0.125 to 0.125
- value_weight: bfloat16 [2048, 2048], P(None, 'tensor'), may hold values from -0.125 to 0.125
- gate_weight: bfloat16 [2048, 2048], P(None, 'tensor'), may hold values from -0.125 to 0.125
- decay_down: bfloat16 [2048, 16], replicated, may hold values from -0.125 to 0.125
- decay_up: bfloat16 [1024, 16], P('tensor'), may hold values from -1.5 to 1.5
- decay_bias: bfloat16 [1024], P('tensor'), may hold values from -3 to 5
- head_gain: bfloat16 [512], replicated, may hold values from 0.5 to 1.5
- out_weight: bfloat16 [2048, 2048], P('tensor'), may hold values from -0.125 to 0.125
- feed_gain: bfloat16 [2048], replicated, may hold values from 0.5 to 1.5
- feed_gate: bfloat16 [2048, 5632], P(None, 'tensor'), may hold values from -0.125 to 0.125
- feed_up: bfloat16 [2048, 5632], P(None, 'tensor'), may hold values from -0.125 to 0.125
- feed_down: bfloat16 [5632, 2048], P('tensor'), may hold values from -0.078125 to 0.078125
Outputs:
- layer_out: bfloat16 [5120, 2048], P('dp')
- token_grad: bfloat16 [5120, 2048], P('dp')
- grad_mixer_gain: float32 [2048], P('dp')
- grad_query: float32 [2048, 1024], P('dp', 'tensor')
- grad_key: float32 [2048, 1024], P('dp', 'tensor')
- grad_value: float32 [2048, 2048], P('dp', 'tensor')
- grad_gate: float32 [2048, 2048], P('dp', 'tensor')
- grad_decay_down: float32 [2048, 16], P('dp')
- grad_decay_up: float32 [4, 256, 16], P('tensor', 'dp')
- grad_decay_bias: float32 [4, 256], P('tensor', 'dp')
- grad_head_gain: float32 [512], P('dp')
- grad_out: float32 [4, 512, 2048], P('tensor', 'dp')
- grad_feed_gain: float32 [2048], P('dp')
- grad_feed_gate: float32 [2048, 5632], P('dp', 'tensor')
- grad_feed_up: float32 [2048, 5632], P('dp', 'tensor')
- grad_feed_down: float32 [4, 1408, 2048], P('tensor', 'dp')
Inputs may be any that keep to these rules, and one draw needn't show every extreme that they name: `token_slots`: the tokens of one sequence fill consecutive positions of one owner, starting at the sum of the lengths before it; every position below the sum of its owner's lengths receives exactly one token and no position above it; the last owner's positions are all filled; of the 640 tokens of one data device's block at most 128 go to one owner, and some owner receives exactly 128 from every block. The lengths of one owner sum to at most 1024, all lengths together to 5120; a length may be 0; some owner holds one sequence of 1024 tokens.
All inputs are finite; a program needn't handle non-finite values.
Results may differ from a plain program's by a relative error of at most 0.019.
Values may be sent and summed in bfloat16 or wider, within the bound.
A program may use at most 256 MiB of HBM per device.

v0:
```python
import jax
import jax.numpy as jnp
from jax import lax
from jax.sharding import PartitionSpec as P

SPAN = 64
OWN_CAP = 1024
epsilon = 1e-06
head_floor = 1.0
highest_precision = lax.Precision.HIGHEST


def segment_ids(lengths_row, row_count):
    boundary = jnp.cumsum(lengths_row)
    position = jnp.arange(row_count, dtype=jnp.int32)
    return jnp.sum((position[:, None] >= boundary[None, :]).astype(jnp.int32), axis=1)


def norm_rows(row_block, gain_row):
    return (
        row_block
        * lax.rsqrt(jnp.mean(row_block * row_block, axis=-1, keepdims=True) + epsilon)
        * gain_row
    )


def gla_head(query_rows, key_rows, value_rows, gate_logits, out_gate, head_gain, segments):
    row_count = query_rows.shape[0]
    key_width = query_rows.shape[1]
    value_width = value_rows.shape[1]
    blocks = row_count // SPAN
    log_decay = (jax.nn.log_sigmoid(gate_logits) / 16.0).reshape(blocks, SPAN, key_width)
    cumulative = jnp.cumsum(log_decay, axis=1)
    span_total = cumulative[:, SPAN - 1, :]
    queries = (query_rows * float(key_width) ** (-0.5)).reshape(blocks, SPAN, key_width)
    key_block = key_rows.reshape(blocks, SPAN, key_width)
    value_vectors = value_rows.reshape(blocks, SPAN, value_width)
    labels = segments.reshape(blocks, SPAN)
    before = jnp.concatenate([jnp.full((1,), -1, jnp.int32), labels[:-1, SPAN - 1]])
    state_carried_in = (labels == before[:, None]).astype(jnp.float32)
    tail_mask = (labels == labels[:, SPAN - 1 :]).astype(jnp.float32)
    position = jnp.arange(SPAN, dtype=jnp.int32)
    allowed = (position[None, :, None] >= position[None, None, :]) & (
        labels[:, :, None] == labels[:, None, :]
    )
    query_decay_scaled = queries * jnp.exp(cumulative)
    key_grown = key_block * jnp.exp(-cumulative)
    key_final = key_block * jnp.exp(span_total[:, None, :] - cumulative) * tail_mask[:, :, None]
    score_matrix = jnp.einsum(
        "nid,njd->nij", query_decay_scaled, key_grown, precision=highest_precision
    )
    score_matrix = jnp.where(allowed, score_matrix, 0.0)
    inside_span_part = jnp.einsum(
        "kgp,kpc->kgc", score_matrix, value_vectors, precision=highest_precision
    )
    updates = jnp.einsum("njd,nje->nde", key_final, value_vectors, precision=highest_precision)

    def advance(carry_state, inputs):
        update, decay_total, keep_flag = inputs
        return (keep_flag * jnp.exp(decay_total)[:, None] * carry_state + update, carry_state)

    _, state_entering_span = lax.scan(
        advance,
        jnp.zeros((key_width, value_width), jnp.float32),
        (updates, span_total, state_carried_in[:, SPAN - 1]),
    )
    cross_span_part = jnp.einsum(
        "rsm,rmh->rsh",
        query_decay_scaled * state_carried_in[:, :, None],
        state_entering_span,
        precision=highest_precision,
    )
    output = (inside_span_part + cross_span_part).reshape(row_count, value_width)
    scaling = lax.rsqrt(jnp.mean(output * output, axis=-1, keepdims=True) + head_floor)
    return output * scaling * head_gain * jax.nn.silu(out_gate)


def contract_rows(left_mat, right_mat):
    return lax.dot_general(
        left_mat, right_mat, (((0,), (0,)), ((), ())), preferred_element_type=jnp.float32
    )


def times_transposed(left_mat, right_mat):
    return lax.dot_general(
        left_mat, right_mat, (((1,), (1,)), ((), ())), preferred_element_type=jnp.float32
    )


def per_device(
    tokens,
    cotangent,
    token_slots,
    lengths,
    mixer_gain,
    query_weight,
    key_weight,
    value_weight,
    gate_weight,
    decay_down,
    decay_up,
    decay_bias,
    head_gain,
    out_weight,
    feed_gain,
    feed_gate,
    feed_up,
    feed_down,
):
    groups = lax.axis_size("dp")
    member = lax.axis_index("dp")
    local_count = tokens.shape[0]
    model_width = tokens.shape[1]
    peer_cap = OWN_CAP // groups
    my_slots = lax.dynamic_slice_in_dim(token_slots, member * local_count, local_count)
    my_owner = my_slots // OWN_CAP
    owner_ids = jnp.arange(groups, dtype=jnp.int32)
    chosen = (my_owner[:, None] == owner_ids[None, :]).astype(jnp.int32)
    rank_in = jnp.sum((jnp.cumsum(chosen, axis=0) - 1) * chosen, axis=1)
    send_pos = my_owner * peer_cap + rank_in

    def pack_rows(row_block):
        buffer_rows = (
            jnp.zeros((groups * peer_cap, model_width), row_block.dtype).at[send_pos].set(row_block)
        )
        return buffer_rows.reshape(groups, peer_cap, model_width)

    arrived = (
        lax.all_to_all(pack_rows(tokens), "dp", split_axis=0, concat_axis=0, tiled=True),
        lax.all_to_all(pack_rows(cotangent), "dp", split_axis=0, concat_axis=0, tiled=True),
    )
    every_owner = (token_slots // OWN_CAP).reshape(groups, local_count)
    is_mine = (every_owner == member).astype(jnp.int32)
    recv_rank = jnp.cumsum(is_mine, axis=1) - 1
    recv_index = jnp.where(
        is_mine > 0, owner_ids[:, None] * peer_cap + recv_rank, groups * peer_cap
    )
    slot_local = (token_slots % OWN_CAP).reshape(groups, local_count)
    slot_map = (
        jnp.full((groups * peer_cap + 1,), OWN_CAP, jnp.int32)
        .at[recv_index.reshape(-1)]
        .set(slot_local.reshape(-1))[: groups * peer_cap]
    )

    def place_rows(row_block):
        flat_block = row_block.reshape(groups * peer_cap, model_width)
        return (
            jnp.zeros((OWN_CAP + 1, model_width), row_block.dtype)
            .at[slot_map]
            .set(flat_block)[:OWN_CAP]
        )

    def unplace_rows(row_block):
        padded = jnp.concatenate([row_block, jnp.zeros((1, model_width), row_block.dtype)], axis=0)
        return padded[slot_map].reshape(groups, peer_cap, model_width)

    def take_back(returned):
        return returned.reshape(groups * peer_cap, model_width)[send_pos]

    owner_rows = place_rows(arrived[0]).astype(jnp.float32)
    upstream = place_rows(arrived[1])
    labels = segment_ids(lengths[0], OWN_CAP)
    mixed_wide, mixer_norm_back = jax.vjp(norm_rows, owner_rows, mixer_gain.astype(jnp.float32))
    normed = mixed_wide.astype(jnp.bfloat16)

    def project(weight):
        return jnp.dot(normed, weight, preferred_element_type=jnp.float32)

    queries = project(query_weight).astype(jnp.bfloat16)
    keys_low = project(key_weight).astype(jnp.bfloat16)
    value_vectors = project(value_weight).astype(jnp.bfloat16)
    gate_pre = project(gate_weight)
    latent = project(decay_down)
    decay_up_wide = decay_up.astype(jnp.float32)
    logits = lax.dot_general(
        latent, decay_up_wide, (((1,), (1,)), ((), ())), precision=highest_precision
    ) + decay_bias.astype(jnp.float32)

    def mixer(query_wide, key_wide, value_wide, logit_wide, gate_wide, gain_wide):
        return gla_head(query_wide, key_wide, value_wide, logit_wide, gate_wide, gain_wide, labels)

    gated_wide, mixer_back = jax.vjp(
        mixer,
        queries.astype(jnp.float32),
        keys_low.astype(jnp.float32),
        value_vectors.astype(jnp.float32),
        logits,
        gate_pre,
        head_gain.astype(jnp.float32),
    )
    gated_low = gated_wide.astype(jnp.bfloat16)
    mixer_partial = jnp.dot(gated_low, out_weight, preferred_element_type=jnp.float32)
    hidden = owner_rows + lax.psum(mixer_partial, "tensor")
    feed_wide, feed_norm_back = jax.vjp(norm_rows, hidden, feed_gain.astype(jnp.float32))
    feed_normed = feed_wide.astype(jnp.bfloat16)
    gate_hidden = jnp.dot(feed_normed, feed_gate, preferred_element_type=jnp.float32)
    up_hidden = jnp.dot(feed_normed, feed_up, preferred_element_type=jnp.float32)
    sigmoid_gate = jax.nn.sigmoid(gate_hidden)
    swish_gate = gate_hidden * sigmoid_gate
    active = (swish_gate * up_hidden).astype(jnp.bfloat16)
    feed_partial = jnp.dot(active, feed_down, preferred_element_type=jnp.float32)
    layer_rows = (
        hidden + lax.psum(feed_partial.astype(jnp.bfloat16), "tensor").astype(jnp.float32)
    ).astype(jnp.bfloat16)
    upstream_wide = upstream.astype(jnp.float32)
    grad_feed_down = contract_rows(active, upstream)
    d_active = times_transposed(upstream, feed_down)
    d_gate_hidden = (
        d_active * up_hidden * sigmoid_gate * (1.0 + gate_hidden * (1.0 - sigmoid_gate))
    ).astype(jnp.bfloat16)
    d_up_hidden = (d_active * swish_gate).astype(jnp.bfloat16)
    grad_feed_gate = contract_rows(feed_normed, d_gate_hidden)
    grad_feed_up = contract_rows(feed_normed, d_up_hidden)
    feed_part = times_transposed(d_gate_hidden, feed_gate) + times_transposed(d_up_hidden, feed_up)
    d_feed = lax.psum(feed_part, "tensor")
    d_hidden_norm, grad_feed_gain = feed_norm_back(d_feed)
    d_hidden = upstream_wide + d_hidden_norm
    d_mixed = d_hidden.astype(jnp.bfloat16)
    gain_term = jnp.zeros((model_width,), jnp.float32)
    grad_out = contract_rows(gated_low, d_mixed)
    d_gated = times_transposed(d_mixed, out_weight)
    d_query, d_key, d_value, d_logits, d_gate, d_head_gain = mixer_back(d_gated)
    d_query_low = d_query.astype(jnp.bfloat16)
    d_key_low = d_key.astype(jnp.bfloat16)
    d_value_low = d_value.astype(jnp.bfloat16)
    d_gate_low = d_gate.astype(jnp.bfloat16)
    grad_decay_bias = jnp.sum(d_logits, axis=0)
    grad_decay_up = lax.dot_general(
        d_logits, latent, (((0,), (0,)), ((), ())), precision=highest_precision
    )
    latent_part = jnp.dot(d_logits, decay_up_wide, precision=highest_precision)
    mixer_part = (
        times_transposed(d_query_low, query_weight)
        + times_transposed(d_key_low, key_weight)
        + times_transposed(d_value_low, value_weight)
        + times_transposed(d_gate_low, gate_weight)
    )
    summed = lax.psum((mixer_part, latent_part, d_head_gain, gain_term), "tensor")
    d_latent = summed[1]
    d_normed = summed[0] + lax.dot_general(
        d_latent,
        decay_down.astype(jnp.float32),
        (((1,), (1,)), ((), ())),
        precision=highest_precision,
    )
    grad_decay_down = lax.dot_general(
        normed.astype(jnp.float32), d_latent, (((0,), (0,)), ((), ())), precision=highest_precision
    )
    grad_query = contract_rows(normed, d_query_low)
    grad_key = contract_rows(normed, d_key_low)
    grad_value = contract_rows(normed, d_value_low)
    grad_gate = contract_rows(normed, d_gate_low)
    d_rows_norm, grad_mixer_gain = mixer_norm_back(d_normed)
    token_rows = (d_hidden + d_rows_norm).astype(jnp.bfloat16)
    shares = (
        lax.psum_scatter(grad_mixer_gain, "dp", scatter_dimension=0, tiled=True),
        lax.psum_scatter(grad_query, "dp", scatter_dimension=0, tiled=True),
        lax.psum_scatter(grad_key, "dp", scatter_dimension=0, tiled=True),
        lax.psum_scatter(grad_value, "dp", scatter_dimension=0, tiled=True),
        lax.psum_scatter(grad_gate, "dp", scatter_dimension=0, tiled=True),
        lax.psum_scatter(grad_decay_down, "dp", scatter_dimension=0, tiled=True),
        lax.psum_scatter(grad_decay_up, "dp", scatter_dimension=0, tiled=True),
        lax.psum_scatter(grad_decay_bias, "dp", scatter_dimension=0, tiled=True),
        lax.psum_scatter(summed[2], "dp", scatter_dimension=0, tiled=True),
        lax.psum_scatter(grad_out, "dp", scatter_dimension=0, tiled=True),
        lax.psum_scatter(grad_feed_gain, "dp", scatter_dimension=0, tiled=True),
        lax.psum_scatter(grad_feed_gate, "dp", scatter_dimension=0, tiled=True),
        lax.psum_scatter(grad_feed_up, "dp", scatter_dimension=0, tiled=True),
        lax.psum_scatter(grad_feed_down, "dp", scatter_dimension=0, tiled=True),
    )
    returned = (
        lax.all_to_all(unplace_rows(layer_rows), "dp", split_axis=0, concat_axis=0, tiled=True),
        lax.all_to_all(unplace_rows(token_rows), "dp", split_axis=0, concat_axis=0, tiled=True),
    )
    layer_out = take_back(returned[0])
    token_grad = take_back(returned[1])
    rank_width = decay_up.shape[1]
    return (
        layer_out,
        token_grad,
        shares[0],
        shares[1],
        shares[2],
        shares[3],
        shares[4],
        shares[5],
        shares[6].reshape(1, -1, rank_width),
        shares[7].reshape(1, -1),
        shares[8],
        shares[9].reshape(1, shares[9].shape[0], model_width),
        shares[10],
        shares[11],
        shares[12],
        shares[13].reshape(1, shares[13].shape[0], model_width),
    )


def solution(mesh):
    placed = (
        P("dp", None),
        P("dp", None),
        P(),
        P("dp", None),
        P(),
        P(None, "tensor"),
        P(None, "tensor"),
        P(None, "tensor"),
        P(None, "tensor"),
        P(),
        P("tensor", None),
        P("tensor"),
        P(),
        P("tensor", None),
        P(),
        P(None, "tensor"),
        P(None, "tensor"),
        P("tensor", None),
    )
    return jax.shard_map(
        per_device,
        mesh=mesh,
        in_specs=placed,
        out_specs=(
            P("dp", None),
            P("dp", None),
            P("dp"),
            P("dp", "tensor"),
            P("dp", "tensor"),
            P("dp", "tensor"),
            P("dp", "tensor"),
            P("dp", None),
            P("tensor", "dp", None),
            P("tensor", "dp"),
            P("dp"),
            P("tensor", "dp", None),
            P("dp"),
            P("dp", "tensor"),
            P("dp", "tensor"),
            P("tensor", "dp", None),
        ),
        check_vma=False,
    )
```

profile of v0, /device:TPU:0, one launch (start us, length us, event | category | flops | bytes accessed | tf_op | source)
XLA Modules:
  0.0 2135.5 jit_solution(18394428422442927344)
XLA Ops:
  11.7 10.5 scatter_custom_fusion.1
  30.1 19.2 scatter_custom_fusion
  50.7 26.0 %all-to-all-done = bf16[8,128,2048]{2,1,0:T(8,128)(2,1)} async-done(((bf16[8,128,2048]{2,1,0:T(8,128)(2,1)}), bf16[8,128,2048]{2,1,0:T(8,128)(2,1)}, u32[]{:S(2)}, u32[]{:S(2)}) %all-to-all-start) | async-done | bytes 4194336 | tf_op jit(solution)/shard_map/all_to_all | solution.py:129
  120.0 61.8 %while.36 = (s32[]{:T(128)}, f32[256,512]{1,0:T(8,128)S(1)}, f32[16,256,512]{2,1,0:T(8,128)}, f32[16,256]{1,0:T(8,128)S(1)}, f32[16,256,1]{1,2,0:T(1,128)}, /*in...) while((s32[]{:T(128)}, f32[256,512]{1,0:T(8,128)S(1)}, ...), condition=%wide.region_13.14_spmd.clone, body=%wide.region_12.13_spmd.clone.sunk | while | flops 524547 | bytes 2629268 | solution.py:62
  182.4 10.8 multiply_reduce_fusion.4
  206.8 10.9 scatter_custom_fusion.3
  222.5 49.1 %all-to-all-done.2 = bf16[8,128,2048]{2,1,0:T(8,128)(2,1)} async-done(((bf16[8,128,2048]{2,1,0:T(8,128)(2,1)}), bf16[8,128,2048]{2,1,0:T(8,128)(2,1)}, u32[]{:S(2)}, u32[]{:S(2)}) %all-to-all-start.2) | async-done | bytes 4194336 | tf_op jit(solution)/shard_map/all_to_all | solution.py:130
  281.6 216.3 %all-reduce.14.cloned.1.call-done = f32[1024,2048]{1,0:T(8,128)} async-done(((f32[1024,2048]{1,0:T(8,128)}), f32[1024,2048]{1,0:T(8,128)}) %all-reduce.14.cloned.1.call-update) | async-done | bytes 8388624 | tf_op jit(solution)/shard_map/psum | solution.py:193
  506.7 11.9 fusion.87
  518.6 10.3 fusion.86
  528.9 15.1 multiply_convert_fusion.1
  554.2 10.9 convolution_add_fusion.1
  565.2 10.9 convolution_convert_fusion
  576.2 278.9 %all-reduce.18.cloned.1.call-done = f32[1024,2048]{1,0:T(8,128)} async-done(((f32[1024,2048]{1,0:T(8,128)}), f32[1024,2048]{1,0:T(8,128)}) %all-reduce.18.cloned.1.call-update) | async-done | bytes 8388624 | tf_op jit(solution)/shard_map/psum | solution.py:215
  862.7 148.8 %all-reduce.16.cloned.1.call-done = bf16[1024,2048]{1,0:T(8,128)(2,1)} async-done(((bf16[1024,2048]{1,0:T(8,128)(2,1)}), bf16[1024,2048]{1,0:T(8,128)(2,1)}) %all-reduce.16.cloned.1.call-update) | async-done | bytes 4194320 | tf_op jit(solution)/shard_map/psum | solution.py:203
  1011.5 12.5 fusion.6
  1068.5 78.5 %while.37 = (s32[]{:T(128)}, f32[256,512]{1,0:T(8,128)S(1)}, f32[16,256,512]{2,1,0:T(8,128)}, f32[16,256]{1,0:T(8,128)S(1)}, f32[16,256,512]{2,1,0:T(8,128)}, /*...) while((s32[]{:T(128)}, f32[256,512]{1,0:T(8,128)S(1)}, ...), condition=%wide.region_25.26_spmd.clone, body=%wide.region_23.25_spmd.clone.sunk | while | flops 786692 | bytes 3157176 | solution.py:62
  1224.4 254.9 %all-reduce.20.cloned.1.call-done = (f32[1024,2048]{1,0:T(8,128)}, f32[1024,16]{0,1:T(8,128)}) async-done(((f32[1024,2048]{1,0:T(8,128)}, f32[1024,16]{0,1:T(8,128)}), (f32[1024,2048]{1,0:T(8,128)}, f32[1024,16]{0,1:T(8,128)})) %all-reduce.20.cloned.1.call-update) | async-done | bytes 8454160 | tf_op jit(solution)/shard_map/psum | solution.py:238
  1484.0 11.4 fusion.12
  1495.6 11.9 fusion.99
  1507.6 11.9 fusion.98
  1524.3 11.8 gather_fusion
  1558.4 11.6 gather_fusion.2
  1570.0 26.1 %all-to-all-done.1 = bf16[8,128,2048]{2,1,0:T(8,128)(2,1)} async-done(((bf16[8,128,2048]{2,1,0:T(8,128)(2,1)}), bf16[8,128,2048]{2,1,0:T(8,128)(2,1)}, u32[]{:S(2)}, u32[]{:S(2)}) %all-to-all-start.1) | async-done | bytes 4194336 | tf_op jit(solution)/shard_map/all_to_all | solution.py:272
  1614.6 60.6 %all-reduce.7 = (f32[2048]{0:T(1024)S(1)}, f32[256]{0:T(256)S(1)}, f32[512]{0:T(512)S(1)}, f32[2048]{0:T(1024)S(1)}) all-reduce(f32[2048]{0:T(1024)S(1)} %get-tuple-element.304, f32[256]{0:T(256)S(1)} %neg.53, f32[512]{0:T(512)S(1)} %copy-done.70, f32[2048]{0:T(1024)S(1)} %copy-done.62), channel_id=2, replica_groups=mesh['dp'=8,'tensor'=4] {'dp'}, use_global_device_ids=true, to_apply=%region_32.33.clone | all-reduce | flops 4864 | bytes 38912
  1676.5 12.4 psum.48
  1708.0 55.7 %reduce-scatter.19.cloned.1.call-done = f32[256,512]{1,0:T(8,128)} async-done(((f32[2048,512]{1,0:T(8,128)}), f32[256,512]{1,0:T(8,128)}) %reduce-scatter.19.cloned.1.call-update) | async-done | bytes 524304 | tf_op jit(solution)/shard_map/reduce_scatter | solution.py:260
  1763.7 55.1 %reduce-scatter.17.cloned.1.call-done = f32[256,512]{1,0:T(8,128)} async-done(((f32[2048,512]{1,0:T(8,128)}), f32[256,512]{1,0:T(8,128)}) %reduce-scatter.17.cloned.1.call-update) | async-done | bytes 524304 | tf_op jit(solution)/shard_map/reduce_scatter | solution.py:259
  1818.8 37.3 %reduce-scatter.21.cloned.1.call-done = f32[256,16]{0,1:T(8,128)} async-done(((f32[2048,16]{0,1:T(8,128)}), f32[256,16]{0,1:T(8,128)}) %reduce-scatter.21.cloned.1.call-update) | async-done | bytes 16400 | tf_op jit(solution)/shard_map/reduce_scatter | solution.py:261
  1856.0 90.8 %reduce-scatter.29.cloned.1.call-done = f32[176,2048]{1,0:T(8,128)} async-done(((f32[1408,2048]{1,0:T(8,128)}), f32[176,2048]{1,0:T(8,128)}) %reduce-scatter.29.cloned.1.call-update) | async-done | bytes 1441808 | tf_op jit(solution)/shard_map/reduce_scatter | solution.py:269
  1946.8 90.9 %reduce-scatter.27.cloned.1.call-done = f32[256,1408]{1,0:T(8,128)} async-done(((f32[2048,1408]{1,0:T(8,128)}), f32[256,1408]{1,0:T(8,128)}) %reduce-scatter.27.cloned.1.call-update) | async-done | bytes 1441808 | tf_op jit(solution)/shard_map/reduce_scatter | solution.py:268
  2037.7 90.8 %reduce-scatter.25.cloned.1.call-done = f32[256,1408]{1,0:T(8,128)} async-done(((f32[2048,1408]{1,0:T(8,128)}), f32[256,1408]{1,0:T(8,128)}) %reduce-scatter.25.cloned.1.call-update) | async-done | bytes 1441808 | tf_op jit(solution)/shard_map/reduce_scatter | solution.py:267
  (532 shorter events, 441.6 us)
Async XLA Ops:
  7.2 186.1 %copy-start = (bf16[2048,512]{1,0:T(8,128)(2,1)S(1)}, bf16[2048,512]{1,0:T(8,128)(2,1)}, u32[]{:S(2)}) copy-start(bf16[2048,512]{1,0:T(8,128)(2,1)} %param.30) | copy-start | bytes 6291460
  11.7 195.1 %copy-start.64 = (s32[640]{0:T(1024)}, s32[640]{0:T(1024)S(1)}, u32[]{:S(2)}) copy-start(s32[640]{0:T(1024)S(1)} %compare_select_fusion.4) | copy-start | bytes 7684
  22.2 54.5 %all-to-all-start = ((bf16[8,128,2048]{2,1,0:T(8,128)(2,1)}), bf16[8,128,2048]{2,1,0:T(8,128)(2,1)}, u32[]{:S(2)}, u32[]{:S(2)}) async-start(bf16[8,128,2048]{2,1,0:T(8,128)(2,1)} %bitcast.199), calls=%async_computation | async-start | bytes 8388608 | tf_op jit(solution)/shard_map/all_to_all | solution.py:129
  27.5 470.4 %all-reduce.14.cloned.1.call-start = ((), (), s32[]{:S(2)}) async-start(), calls=%async_computation.14 | async-start | bytes 16777216 | tf_op jit(solution)/shard_map/psum | solution.py:193
  28.0 76.0 %copy-start.41 = (s32[16,64]{1,0:T(8,128)}, s32[16,64]{1,0:T(8,128)S(1)}, u32[]{:S(2)}) copy-start(s32[16,64]{1,0:T(8,128)S(1)} %eq.92) | copy-start | bytes 12292
  28.0 62.0 %copy-start.51 = (f32[2048]{0:T(1024)}, f32[2048]{0:T(1024)S(1)}, u32[]{:S(2)}) copy-start(f32[2048]{0:T(1024)S(1)} %convert_element_type.127) | copy-start | bytes 24580
  49.7 54.3 %copy-start.55 = (pred[64,64]{1,0:T(8,128)(4,1)}, pred[64,64]{1,0:T(8,128)(4,1)S(1)}, u32[]{:S(2)}) copy-start(pred[64,64]{1,0:T(8,128)(4,1)S(1)} %iota_compare_fusion) | copy-start | bytes 12292
  49.9 59.0 %copy-start.53 = (f32[16,64]{1,0:T(8,128)}, f32[16,64]{1,0:T(8,128)S(1)}, u32[]{:S(2)}) copy-start(f32[16,64]{1,0:T(8,128)S(1)} %get-tuple-element.369) | copy-start | bytes 12292
  217.7 53.8 %all-to-all-start.2 = ((bf16[8,128,2048]{2,1,0:T(8,128)(2,1)}), bf16[8,128,2048]{2,1,0:T(8,128)(2,1)}, u32[]{:S(2)}, u32[]{:S(2)}) async-start(bf16[8,128,2048]{2,1,0:T(8,128)(2,1)} %bitcast.200), calls=%async_computation.2 | async-start | bytes 8388608 | tf_op jit(solution)/shard_map/all_to_all | solution.py:130
  222.4 632.7 %all-reduce.18.cloned.1.call-start = ((), (), s32[]{:S(2)}) async-start(), calls=%async_computation.16 | async-start | bytes 16777216 | tf_op jit(solution)/shard_map/psum | solution.py:215
  506.7 22.2 %slice-start.6 = ((s8[4227072]{0:T(1024)(128)(4,1)}), s8[4194304]{0:T(1024)(128)(4,1)S(1)}, s32[]{:S(2)}) async-start(s8[4227072]{0:T(1024)(128)(4,1)} %bitcast.191), calls=%async_computation.34 | async-start | bytes 8388608
  565.1 446.4 %all-reduce.16.cloned.1.call-start = ((), (), s32[]{:S(2)}) async-start(), calls=%async_computation.15 | async-start | bytes 8388608 | tf_op jit(solution)/shard_map/psum | solution.py:203
  576.1 903.2 %all-reduce.20.cloned.1.call-start = ((), (), s32[]{:S(2)}) async-start(), calls=%async_computation.27 | async-start | bytes 16908288 | tf_op jit(solution)/shard_map/psum | solution.py:238
  1032.9 25.5 %copy-start.34 = (bf16[1024,512]{1,0:T(8,128)(2,1)}, bf16[1024,512]{1,0:T(8,128)(2,1)S(1)}, u32[]{:S(2)}) copy-start(bf16[1024,512]{1,0:T(8,128)(2,1)S(1)} %get-tuple-element.363) | copy-start | bytes 3145732
  1033.0 16.1 slice-start.2
  1068.5 78.5 %copy-start.14 = (bf16[1024,256]{1,0:T(8,128)(2,1)S(1)}, bf16[1024,256]{1,0:T(8,128)(2,1)}, u32[]{:S(2)}) copy-start(bf16[1024,256]{1,0:T(8,128)(2,1)} %copy-done.12) | copy-start | bytes 1572868
  1068.5 78.5 %copy-start.44 = (f32[16,256]{1,0:T(8,128)S(1)}, f32[16,256]{1,0:T(8,128)}, u32[]{:S(2)}) copy-start(f32[16,256]{1,0:T(8,128)} %copy-done.43) | copy-start | bytes 49156
  1068.5 78.5 %copy-start.54 = (f32[16,64]{1,0:T(8,128)S(1)}, f32[16,64]{1,0:T(8,128)}, u32[]{:S(2)}) copy-start(f32[16,64]{1,0:T(8,128)} %copy-done.53) | copy-start | bytes 12292
  1186.5 417.0 %reduce-scatter.31.cloned.1.call-start = ((), (), s32[]{:S(2)}) async-start(), calls=%async_computation.26 | async-start | bytes 147456
  1189.8 509.6 %reduce-scatter.15.cloned.1.call-start = ((), (), s32[]{:S(2)}) async-start(), calls=%async_computation.18 | async-start | bytes 2359296 | tf_op jit(solution)/shard_map/reduce_scatter | solution.py:258
  1195.6 503.8 %reduce-scatter.13.cloned.1.call-start = ((), (), s32[]{:S(2)}) async-start(), calls=%async_computation.17 | async-start | bytes 2359296 | tf_op jit(solution)/shard_map/reduce_scatter | solution.py:257
  1200.6 507.4 %reduce-scatter.23.cloned.1.call-start = ((), (), s32[]{:S(2)}) async-start(), calls=%async_computation.22 | async-start | bytes 4718592 | tf_op jit(solution)/shard_map/reduce_scatter | solution.py:265
  1208.7 555.0 %reduce-scatter.19.cloned.1.call-start = ((), (), s32[]{:S(2)}) async-start(), calls=%async_computation.20 | async-start | bytes 4718592 | tf_op jit(solution)/shard_map/reduce_scatter | solution.py:260
  1216.6 602.2 %reduce-scatter.17.cloned.1.call-start = ((), (), s32[]{:S(2)}) async-start(), calls=%async_computation.19 | async-start | bytes 4718592 | tf_op jit(solution)/shard_map/reduce_scatter | solution.py:259
  1224.4 631.7 %reduce-scatter.21.cloned.1.call-start = ((), (), s32[]{:S(2)}) async-start(), calls=%async_computation.21 | async-start | bytes 147456 | tf_op jit(solution)/shard_map/reduce_scatter | solution.py:261
  1483.9 462.9 %reduce-scatter.29.cloned.1.call-start = ((), (), s32[]{:S(2)}) async-start(), calls=%async_computation.25 | async-start | bytes 12976128 | tf_op jit(solution)/shard_map/reduce_scatter | solution.py:269
  1495.4 542.3 %reduce-scatter.27.cloned.1.call-start = ((), (), s32[]{:S(2)}) async-start(), calls=%async_computation.24 | async-start | bytes 12976128 | tf_op jit(solution)/shard_map/reduce_scatter | solution.py:268
  1507.6 620.9 %reduce-scatter.25.cloned.1.call-start = ((), (), s32[]{:S(2)}) async-start(), calls=%async_computation.23 | async-start | bytes 12976128 | tf_op jit(solution)/shard_map/reduce_scatter | solution.py:267
  1536.1 13.8 slice-start
  1536.1 60.0 %all-to-all-start.1 = ((bf16[8,128,2048]{2,1,0:T(8,128)(2,1)}), bf16[8,128,2048]{2,1,0:T(8,128)(2,1)}, u32[]{:S(2)}, u32[]{:S(2)}) async-start(bf16[8,128,2048]{2,1,0:T(8,128)(2,1)} %bitcast.198), calls=%async_computation.1 | async-start | bytes 8388608 | tf_op jit(solution)/shard_map/all_to_all | solution.py:272
  1596.1 93.4 %all-to-all-start.3 = ((bf16[8,128,2048]{2,1,0:T(8,128)(2,1)}), bf16[8,128,2048]{2,1,0:T(8,128)(2,1)}, u32[]{:S(2)}, u32[]{:S(2)}) async-start(bf16[8,128,2048]{2,1,0:T(8,128)(2,1)} %bitcast.197), calls=%async_computation.3 | async-start | bytes 8388608 | tf_op jit(solution)/shard_map/all_to_all | solution.py:273
  1689.5 438.9 %copy-start.1 = (bf16[2048,512]{1,0:T(8,128)(2,1)S(1)}, bf16[2048,512]{1,0:T(8,128)(2,1)}, u32[]{:S(2)}) copy-start(bf16[2048,512]{1,0:T(8,128)(2,1)} %param.30) | copy-start | bytes 6291460
  (77 other events, 461.3 us)
Sparse Core Ops, SparseCore 0:
  206.9 290.9 all-reduce.13
  565.2 289.8 all-reduce.17
  857.5 153.9 all-reduce.15
  1186.6 292.6 all-reduce.19
  1482.4 32.3 reduce-scatter.30
  1518.5 60.9 reduce-scatter.14
  1583.7 69.8 reduce-scatter.12
  1657.5 50.4 reduce-scatter.22
  1712.3 51.3 reduce-scatter.18
  1767.4 51.2 reduce-scatter.16
  1822.6 33.3 reduce-scatter.20
  1859.9 86.8 reduce-scatter.28
  1950.9 86.7 reduce-scatter.26
  2041.6 86.7 reduce-scatter.24
where the time goes:
time: 2150 us; the launch traced here: 2140 us
  waiting for transfers between devices  1430 us (67%)
  matrix products  267 us (12%)
  local copies, waits for them, and re-layouts  168 us (8%)
  other arithmetic  159 us (7%)
  blocking collectives  73 us (3%)
    psum x1, waiting for transfers between devices, per_device(): d_feed = lax.psum(feed_part, 'tensor')  279 us
    psum x1, waiting for transfers between devices, per_device(): lax.psum((mixer_part, latent_part, d_head_gain, gain_term), 'tensor')  255 us
    psum x1, waiting for transfers between devices, per_device(): hidden = owner_rows + lax.psum(mixer_partial, 'tensor')  216 us
    psum x1, waiting for transfers between devices, per_device(): lax.psum(feed_partial.astype(jnp.bfloat16), 'tensor').astype(jnp.float32)  149 us
    reduce_scatter x1, waiting for transfers between devices, per_device(): lax.psum_scatter(grad_feed_up, 'dp', scatter_dimension=0, tiled=True)  90.9 us
    reduce_scatter x1, waiting for transfers between devices, per_device(): lax.psum_scatter(grad_feed_down, 'dp', scatter_dimension=0, tiled=True)  90.8 us
    reduce_scatter x1, waiting for transfers between devices, per_device(): lax.psum_scatter(grad_feed_gate, 'dp', scatter_dimension=0, tiled=True)  90.8 us
    dot_general x8, matrix products, contract_rows(): lax.dot_general(left_mat, right_mat, (((0,), (0,)), ((), ())), preferred_...  66.8 us
  transfers between devices with their start and end apart: 18, of which 14 were waited for; matrix products, arithmetic and copies ran while one was open for 10% of the time, Pallas kernels for 0%

commit v1 on v0

--- a/solution.py
+++ b/solution.py
@@ -8,6 +8,16 @@
 epsilon = 1e-06
 head_floor = 1.0
 highest_precision = lax.Precision.HIGHEST
+
+
+def cover_numbers(vector, along_axis):
+    n_parts = lax.psum(1, along_axis)
+    a_next, prior = (vector, 0)
+    while 1 << prior < n_parts:
+        right_arr = lax.ppermute(a_next, along_axis, [(m, m ^ 1 << prior) for m in range(n_parts)])
+        a_next = a_next + right_arr
+        prior = prior + 1
+    return a_next
 
 
 def segment_ids(lengths_row, row_count):
@@ -212,7 +222,7 @@
     grad_feed_gate = contract_rows(feed_normed, d_gate_hidden)
     grad_feed_up = contract_rows(feed_normed, d_up_hidden)
     feed_part = times_transposed(d_gate_hidden, feed_gate) + times_transposed(d_up_hidden, feed_up)
-    d_feed = lax.psum(feed_part, "tensor")
+    d_feed = cover_numbers(feed_part, "tensor")
     d_hidden_norm, grad_feed_gain = feed_norm_back(d_feed)
     d_hidden = upstream_wide + d_hidden_norm
     d_mixed = d_hidden.astype(jnp.bfloat16)

time: 2150 us -> 2440 us (1.13)
  waiting for transfers between devices: 1430 us -> 1640 us
  other arithmetic: 159 us -> 241 us
    ppermute x0 -> x2, waiting for transfers between devices: none -> 668 us  [cover_numbers(): lax.ppermute(a_next, along_axis, [(m, m ^ 1 << prior) for m in range(n_pa...]
    psum x1 -> x0, waiting for transfers between devices: 279 us -> none  [per_device(): d_feed = lax.psum(feed_part, 'tensor')]
    psum x1, waiting for transfers between devices: 149 us -> 0.01 us  [per_device(): lax.psum(feed_partial.astype(jnp.bfloat16), 'tensor').astype(jnp.float32)]
    reduce_scatter x1, waiting for transfers between devices: 90.8 us -> 3.78 us  [per_device(): lax.psum_scatter(grad_feed_gate, 'dp', scatter_dimension=0, tiled=True)]
    psum x1, waiting for transfers between devices: 255 us -> 197 us  [per_device(): lax.psum((mixer_part, latent_part, d_head_gain, gain_term), 'tensor')]
    reduce_scatter x1, waiting for transfers between devices: 8.56 us -> 55.7 us  [per_device(): lax.psum_scatter(grad_out, 'dp', scatter_dimension=0, tiled=True)]
    reduce_scatter x1, waiting for transfers between devices: 0.01 us -> 45.5 us  [per_device(): lax.psum_scatter(grad_key, 'dp', scatter_dimension=0, tiled=True)]
    reduce_scatter x1, waiting for transfers between devices: 0.01 us -> 45.1 us  [per_device(): lax.psum_scatter(grad_query, 'dp', scatter_dimension=0, tiled=True)]
  transfers between devices with their start and end apart: 18 -> 19, of which waited for: 14 -> 15; matrix products, arithmetic and copies ran while one was open for 10% -> 9% of each run, Pallas kernels for 0% -> 0%
where the time goes in v1:
time: 2440 us; the launch traced here: 2420 us
  waiting for transfers between devices  1640 us (67%)
  matrix products  263 us (11%)
  other arithmetic  241 us (10%)
  local copies, waits for them, and re-layouts  171 us (7%)
  blocking collectives  70 us (3%)
    ppermute x2, waiting for transfers between devices, cover_numbers(): lax.ppermute(a_next, along_axis, [(m, m ^ 1 << prior) for m in range(n_pa...  668 us
    psum x1, waiting for transfers between devices, per_device(): hidden = owner_rows + lax.psum(mixer_partial, 'tensor')  217 us
    psum x1, waiting for transfers between devices, per_device(): lax.psum((mixer_part, latent_part, d_head_gain, gain_term), 'tensor')  197 us
    reduce_scatter x1, waiting for transfers between devices, per_device(): lax.psum_scatter(grad_feed_down, 'dp', scatter_dimension=0, tiled=True)  90.9 us
    reduce_scatter x1, waiting for transfers between devices, per_device(): lax.psum_scatter(grad_feed_up, 'dp', scatter_dimension=0, tiled=True)  90.8 us
    dynamic_update_slice x48, other arithmetic, gla_head(): lax.scan(advance, jnp.zeros((key_width, value_width), jnp.float32), (upda...  77.9 us
    dot_general x8, matrix products, contract_rows(): lax.dot_general(left_mat, right_mat, (((0,), (0,)), ((), ())), preferred_...  67.7 us
    dot_general x8, matrix products, times_transposed(): lax.dot_general(left_mat, right_mat, (((1,), (1,)), ((), ())), preferred_...  61.5 us
  transfers between devices with their start and end apart: 19, of which 15 were waited for; matrix products, arithmetic and copies ran while one was open for 9% of the time, Pallas kernels for 0%

profile of v1, /device:TPU:0, one launch (start us, length us, event | category | flops | bytes accessed | tf_op | source)
XLA Modules:
  0.0 2422.0 jit_solution(17156740587101785855)
XLA Ops:
  11.7 10.5 scatter_custom_fusion.1
  30.1 19.2 scatter_custom_fusion
  50.7 26.0 %all-to-all-done = bf16[8,128,2048]{2,1,0:T(8,128)(2,1)} async-done(((bf16[8,128,2048]{2,1,0:T(8,128)(2,1)}), bf16[8,128,2048]{2,1,0:T(8,128)(2,1)}, u32[]{:S(2)}, u32[]{:S(2)}) %all-to-all-start) | async-done | bytes 4194336 | tf_op jit(solution)/shard_map/all_to_all | solution.py:139
  76.7 10.4 scatter_custom_fusion.2
  112.4 92.5 %while.36 = (s32[]{:T(128)}, f32[256,512]{1,0:T(8,128)}, f32[16,256,512]{2,1,0:T(8,128)}, f32[16,256]{1,0:T(8,128)S(1)}, f32[16,256,1]{1,2,0:T(1,128)}, /*index=...) while((s32[]{:T(128)}, f32[256,512]{1,0:T(8,128)}, ...), condition=%wide.region_13.14_spmd.clone, body=%wide.region_12.13_spmd.clone.sunk | while | flops 524547 | bytes 2630276 | solution.py:72
  234.1 10.5 scatter_custom_fusion.3
  249.3 49.1 %all-to-all-done.2 = bf16[8,128,2048]{2,1,0:T(8,128)(2,1)} async-done(((bf16[8,128,2048]{2,1,0:T(8,128)(2,1)}), bf16[8,128,2048]{2,1,0:T(8,128)(2,1)}, u32[]{:S(2)}, u32[]{:S(2)}) %all-to-all-start.2) | async-done | bytes 4194336 | tf_op jit(solution)/shard_map/all_to_all | solution.py:140
  308.5 216.7 %all-reduce.13.cloned.1.call-done = f32[1024,2048]{1,0:T(8,128)} async-done(((f32[1024,2048]{1,0:T(8,128)}), f32[1024,2048]{1,0:T(8,128)}) %all-reduce.13.cloned.1.call-update) | async-done | bytes 8388624 | tf_op jit(solution)/shard_map/psum | solution.py:203
  534.0 11.9 fusion.86
  556.2 15.1 multiply_convert_fusion.1
  593.3 182.3 %collective-permute-done = f32[1024,2048]{1,0:T(8,128)} collective-permute-done((f32[1024,2048]{1,0:T(8,128)S(1)}, f32[1024,2048]{1,0:T(8,128)}, u32[]{:S(2)}, u32[]{:S(2)}) %collective-permute-start) | collective-permute-done | bytes 8388640 | tf_op jit(solution)/shard_map/ppermute | solution.py:17
  775.6 11.8 add.235
  788.9 11.0 convolution_convert_fusion
  800.0 485.3 %collective-permute-done.1 = f32[1024,2048]{1,0:T(8,128)} collective-permute-done((f32[1024,2048]{1,0:T(8,128)}, f32[1024,2048]{1,0:T(8,128)}, u32[]{:S(2)}, u32[]{:S(2)}) %collective-permute-start.1) | collective-permute-done | bytes 8388640 | tf_op jit(solution)/shard_map/ppermute | solution.py:17
  1285.2 10.7 multiply_reduce_fusion
  1296.0 18.3 fusion.6
  1354.2 109.1 %while.37 = (s32[]{:T(128)}, f32[256,512]{1,0:T(8,128)}, f32[16,256,512]{2,1,0:T(8,128)}, f32[16,256]{1,0:T(8,128)S(1)}, f32[16,256,512]{2,1,0:T(8,128)}, /*inde...) while((s32[]{:T(128)}, f32[256,512]{1,0:T(8,128)}, ...), condition=%wide.region_24.25_spmd.clone, body=%wide.region_22.24_spmd.clone.sunk | while | flops 786692 | bytes 3157168 | solution.py:72
  1512.6 12.7 fusion.98
  1525.4 11.9 fusion.99
  1537.4 11.7 fusion.12
  1580.9 11.7 gather_fusion
  1604.6 197.4 %all-reduce.17.cloned.1.call-done = (f32[1024,2048]{1,0:T(8,128)}, f32[1024,16]{0,1:T(8,128)}) async-done(((f32[1024,2048]{1,0:T(8,128)}, f32[1024,16]{0,1:T(8,128)}), (f32[1024,2048]{1,0:T(8,128)}, f32[1024,16]{0,1:T(8,128)})) %all-reduce.17.cloned.1.call-update) | async-done | bytes 8454160 | tf_op jit(solution)/shard_map/psum | solution.py:248
  1819.6 11.6 gather_fusion.2
  1854.5 61.2 %all-reduce.7 = (f32[2048]{0:T(1024)S(1)}, f32[256]{0:T(256)S(1)}, f32[512]{0:T(512)S(1)}, f32[2048]{0:T(1024)S(1)}) all-reduce(f32[2048]{0:T(1024)S(1)} %get-tuple-element.304, f32[256]{0:T(256)S(1)} %neg.53, f32[512]{0:T(512)S(1)} %copy-done.73, f32[2048]{0:T(1024)S(1)} %copy-done.65), channel_id=2, replica_groups=mesh['dp'=8,'tensor'=4] {'dp'}, use_global_device_ids=true, to_apply=%region_31.32.clone | all-reduce | flops 4864 | bytes 38912
  1939.9 90.8 %reduce-scatter.27.cloned.1.call-done = f32[256,1408]{1,0:T(8,128)} async-done(((f32[2048,1408]{1,0:T(8,128)}), f32[256,1408]{1,0:T(8,128)}) %reduce-scatter.27.cloned.1.call-update) | async-done | bytes 1441808 | tf_op jit(solution)/shard_map/reduce_scatter | solution.py:278
  2030.7 90.9 %reduce-scatter.29.cloned.1.call-done = f32[176,2048]{1,0:T(8,128)} async-done(((f32[1408,2048]{1,0:T(8,128)}), f32[176,2048]{1,0:T(8,128)}) %reduce-scatter.29.cloned.1.call-update) | async-done | bytes 1441808 | tf_op jit(solution)/shard_map/reduce_scatter | solution.py:279
  2121.6 45.1 %reduce-scatter.13.cloned.1.call-done = f32[256,256]{1,0:T(8,128)} async-done(((f32[2048,256]{1,0:T(8,128)}), f32[256,256]{1,0:T(8,128)}) %reduce-scatter.13.cloned.1.call-update) | async-done | bytes 262160 | tf_op jit(solution)/shard_map/reduce_scatter | solution.py:267
  2166.6 45.5 %reduce-scatter.15.cloned.1.call-done = f32[256,256]{1,0:T(8,128)} async-done(((f32[2048,256]{1,0:T(8,128)}), f32[256,256]{1,0:T(8,128)}) %reduce-scatter.15.cloned.1.call-update) | async-done | bytes 262160 | tf_op jit(solution)/shard_map/reduce_scatter | solution.py:268
  2212.1 55.1 %reduce-scatter.17.cloned.1.call-done = f32[256,512]{1,0:T(8,128)} async-done(((f32[2048,512]{1,0:T(8,128)}), f32[256,512]{1,0:T(8,128)}) %reduce-scatter.17.cloned.1.call-update) | async-done | bytes 524304 | tf_op jit(solution)/shard_map/reduce_scatter | solution.py:269
  2267.3 55.7 %reduce-scatter.23.cloned.1.call-done = f32[64,2048]{1,0:T(8,128)} async-done(((f32[512,2048]{1,0:T(8,128)}), f32[64,2048]{1,0:T(8,128)}) %reduce-scatter.23.cloned.1.call-update) | async-done | bytes 524304 | tf_op jit(solution)/shard_map/reduce_scatter | solution.py:275
  2322.9 55.1 %reduce-scatter.19.cloned.1.call-done = f32[256,512]{1,0:T(8,128)} async-done(((f32[2048,512]{1,0:T(8,128)}), f32[256,512]{1,0:T(8,128)}) %reduce-scatter.19.cloned.1.call-update) | async-done | bytes 524304 | tf_op jit(solution)/shard_map/reduce_scatter | solution.py:270
  2378.0 37.3 %reduce-scatter.21.cloned.1.call-done = f32[256,16]{0,1:T(8,128)} async-done(((f32[2048,16]{0,1:T(8,128)}), f32[256,16]{0,1:T(8,128)}) %reduce-scatter.21.cloned.1.call-update) | async-done | bytes 16400 | tf_op jit(solution)/shard_map/reduce_scatter | solution.py:271
  (547 shorter events, 521.4 us)
Async XLA Ops:
  7.2 212.9 %copy-start = (bf16[2048,512]{1,0:T(8,128)(2,1)S(1)}, bf16[2048,512]{1,0:T(8,128)(2,1)}, u32[]{:S(2)}) copy-start(bf16[2048,512]{1,0:T(8,128)(2,1)} %param.30) | copy-start | bytes 6291460
  11.7 222.4 %copy-start.67 = (s32[640]{0:T(1024)}, s32[640]{0:T(1024)S(1)}, u32[]{:S(2)}) copy-start(s32[640]{0:T(1024)S(1)} %compare_select_fusion.4) | copy-start | bytes 7684
  22.2 54.5 %all-to-all-start = ((bf16[8,128,2048]{2,1,0:T(8,128)(2,1)}), bf16[8,128,2048]{2,1,0:T(8,128)(2,1)}, u32[]{:S(2)}, u32[]{:S(2)}) async-start(bf16[8,128,2048]{2,1,0:T(8,128)(2,1)} %bitcast.198), calls=%async_computation | async-start | bytes 8388608 | tf_op jit(solution)/shard_map/all_to_all | solution.py:139
  27.5 497.7 %all-reduce.13.cloned.1.call-start = ((), (), s32[]{:S(2)}) async-start(), calls=%async_computation.14 | async-start | bytes 16777216 | tf_op jit(solution)/shard_map/psum | solution.py:203
  30.1 180.4 %copy-start.40 = (s32[16,64]{1,0:T(8,128)}, s32[16,64]{1,0:T(8,128)S(1)}, u32[]{:S(2)}) copy-start(s32[16,64]{1,0:T(8,128)S(1)} %eq.92) | copy-start | bytes 12292
  49.7 160.9 %copy-start.56 = (pred[64,64]{1,0:T(8,128)(4,1)}, pred[64,64]{1,0:T(8,128)(4,1)S(1)}, u32[]{:S(2)}) copy-start(pred[64,64]{1,0:T(8,128)(4,1)S(1)} %iota_compare_fusion) | copy-start | bytes 12292
  49.9 163.5 %copy-start.49 = (f32[16,64]{1,0:T(8,128)}, f32[16,64]{1,0:T(8,128)S(1)}, u32[]{:S(2)}) copy-start(f32[16,64]{1,0:T(8,128)S(1)} %get-tuple-element.370) | copy-start | bytes 12292
  97.2 113.4 %copy-start.2 = (f32[16,64,256]{2,0,1:T(8,128)}, f32[16,64,256]{2,0,1:T(8,128)S(1)}, u32[]{:S(2)}) copy-start(f32[16,64,256]{2,0,1:T(8,128)S(1)} %fusion.51) | copy-start | bytes 3145732
  244.6 53.8 %all-to-all-start.2 = ((bf16[8,128,2048]{2,1,0:T(8,128)(2,1)}), bf16[8,128,2048]{2,1,0:T(8,128)(2,1)}, u32[]{:S(2)}, u32[]{:S(2)}) async-start(bf16[8,128,2048]{2,1,0:T(8,128)(2,1)} %bitcast.199), calls=%async_computation.2 | async-start | bytes 8388608 | tf_op jit(solution)/shard_map/all_to_all | solution.py:140
  249.3 1046.7 %all-reduce.15.cloned.1.call-start = ((), (), s32[]{:S(2)}) async-start(), calls=%async_computation.15 | async-start | bytes 8388608 | tf_op jit(solution)/shard_map/psum | solution.py:213
  593.3 195.5 %copy-start.83 = (bf16[1024,1408]{1,0:T(8,128)(2,1)S(1)}, bf16[1024,1408]{1,0:T(8,128)(2,1)}, u32[]{:S(2)}) copy-start(bf16[1024,1408]{1,0:T(8,128)(2,1)} %get-tuple-element.359) | copy-start | bytes 8650756
  593.3 182.3 %collective-permute-start = (f32[1024,2048]{1,0:T(8,128)S(1)}, f32[1024,2048]{1,0:T(8,128)}, u32[]{:S(2)}, u32[]{:S(2)}) collective-permute-start(f32[1024,2048]{1,0:T(8,128)S(1)} %convolution_add_fusion.1), channel_id=1, source_target_pairs={{0,1},{1,0},{2,3},{3,2},{4,5},{5,4},{6,7},{7,6},{8,9},{9,8},{10,11... | collective-permute-start | bytes 25165832 | tf_op jit(solution)/shard_map/ppermute | solution.py:17
  787.4 497.8 %collective-permute-start.1 = (f32[1024,2048]{1,0:T(8,128)}, f32[1024,2048]{1,0:T(8,128)}, u32[]{:S(2)}, u32[]{:S(2)}) collective-permute-start(f32[1024,2048]{1,0:T(8,128)} %add.235), channel_id=1, source_target_pairs={{0,2},{1,3},{2,0},{3,1},{4,6},{5,7},{6,4},{7,5},{8,10},{9,11},{10,... | collective-permute-start | bytes 25165832 | tf_op jit(solution)/shard_map/ppermute | solution.py:17
  799.9 1002.1 %all-reduce.17.cloned.1.call-start = ((), (), s32[]{:S(2)}) async-start(), calls=%async_computation.26 | async-start | bytes 16908288 | tf_op jit(solution)/shard_map/psum | solution.py:248
  1354.2 109.1 %copy-start.43 = (f32[16,256]{1,0:T(8,128)S(1)}, f32[16,256]{1,0:T(8,128)}, u32[]{:S(2)}) copy-start(f32[16,256]{1,0:T(8,128)} %copy-done.42) | copy-start | bytes 49156
  1354.2 109.1 %copy-start.55 = (f32[16,64]{1,0:T(8,128)S(1)}, f32[16,64]{1,0:T(8,128)}, u32[]{:S(2)}) copy-start(f32[16,64]{1,0:T(8,128)} %copy-done.54) | copy-start | bytes 12292
  1508.9 334.4 %reduce-scatter.31.cloned.1.call-start = ((), (), s32[]{:S(2)}) async-start(), calls=%async_computation.25 | async-start | bytes 147456
  1512.6 427.3 %reduce-scatter.25.cloned.1.call-start = ((), (), s32[]{:S(2)}) async-start(), calls=%async_computation.22 | async-start | bytes 12976128 | tf_op jit(solution)/shard_map/reduce_scatter | solution.py:277
  1525.3 505.3 %reduce-scatter.27.cloned.1.call-start = ((), (), s32[]{:S(2)}) async-start(), calls=%async_computation.23 | async-start | bytes 12976128 | tf_op jit(solution)/shard_map/reduce_scatter | solution.py:278
  1537.4 584.2 %reduce-scatter.29.cloned.1.call-start = ((), (), s32[]{:S(2)}) async-start(), calls=%async_computation.24 | async-start | bytes 12976128 | tf_op jit(solution)/shard_map/reduce_scatter | solution.py:279
  1549.1 617.6 %reduce-scatter.13.cloned.1.call-start = ((), (), s32[]{:S(2)}) async-start(), calls=%async_computation.16 | async-start | bytes 2359296 | tf_op jit(solution)/shard_map/reduce_scatter | solution.py:267
  1554.9 657.2 %reduce-scatter.15.cloned.1.call-start = ((), (), s32[]{:S(2)}) async-start(), calls=%async_computation.17 | async-start | bytes 2359296 | tf_op jit(solution)/shard_map/reduce_scatter | solution.py:268
  1559.9 707.4 %reduce-scatter.17.cloned.1.call-start = ((), (), s32[]{:S(2)}) async-start(), calls=%async_computation.18 | async-start | bytes 4718592 | tf_op jit(solution)/shard_map/reduce_scatter | solution.py:269
  1566.9 756.1 %reduce-scatter.23.cloned.1.call-start = ((), (), s32[]{:S(2)}) async-start(), calls=%async_computation.21 | async-start | bytes 4718592 | tf_op jit(solution)/shard_map/reduce_scatter | solution.py:275
  1592.6 238.6 %all-to-all-start.1 = ((bf16[8,128,2048]{2,1,0:T(8,128)(2,1)}), bf16[8,128,2048]{2,1,0:T(8,128)(2,1)}, u32[]{:S(2)}, u32[]{:S(2)}) async-start(bf16[8,128,2048]{2,1,0:T(8,128)(2,1)} %bitcast.197), calls=%async_computation.1 | async-start | bytes 8388608 | tf_op jit(solution)/shard_map/all_to_all | solution.py:282
  1597.7 780.3 %reduce-scatter.19.cloned.1.call-start = ((), (), s32[]{:S(2)}) async-start(), calls=%async_computation.19 | async-start | bytes 4718592 | tf_op jit(solution)/shard_map/reduce_scatter | solution.py:270
  1597.8 213.3 %slice-start = ((s8[4227072]{0:T(1024)(128)(4,1)}), s8[32768]{0:T(1024)(128)(4,1)S(1)}, s32[]{:S(2)}) async-start(s8[4227072]{0:T(1024)(128)(4,1)} %bitcast.171), calls=%async_computation.27 | async-start | bytes 65536
  1604.6 197.5 %copy-start.47 = (bf16[2048,16]{0,1:T(8,128)(2,1)S(1)}, bf16[2048,16]{0,1:T(8,128)(2,1)}, u32[]{:S(2)}) copy-start(bf16[2048,16]{0,1:T(8,128)(2,1)} %param.31) | copy-start | bytes 196612
  1604.6 197.5 %copy-start.53 = (f32[2048]{0:T(1024)S(1)}, f32[2048]{0:T(1024)}, u32[]{:S(2)}) copy-start(f32[2048]{0:T(1024)} %copy-done.52) | copy-start | bytes 24580
  1604.6 197.5 %copy-start.59 = (f32[1024]{0:T(1024)S(1)}, f32[1024]{0:T(1024)}, u32[]{:S(2)}) copy-start(f32[1024]{0:T(1024)} %copy-done.58) | copy-start | bytes 12292
  1831.2 95.2 %all-to-all-start.3 = ((bf16[8,128,2048]{2,1,0:T(8,128)(2,1)}), bf16[8,128,2048]{2,1,0:T(8,128)(2,1)}, u32[]{:S(2)}, u32[]{:S(2)}) async-start(bf16[8,128,2048]{2,1,0:T(8,128)(2,1)} %bitcast.196), calls=%async_computation.3 | async-start | bytes 8388608 | tf_op jit(solution)/shard_map/all_to_all | solution.py:283
  1835.9 579.4 %reduce-scatter.21.cloned.1.call-start = ((), (), s32[]{:S(2)}) async-start(), calls=%async_computation.20 | async-start | bytes 147456 | tf_op jit(solution)/shard_map/reduce_scatter | solution.py:271
  (84 other events, 628.4 us)
Sparse Core Ops, SparseCore 0:
  234.2 290.9 all-reduce.12
  800.0 384.5 all-reduce.14
  1509.0 292.9 all-reduce.16
  1805.2 32.3 reduce-scatter.30
  1841.5 98.3 reduce-scatter.24
  1943.8 86.7 reduce-scatter.26
  2034.7 86.7 reduce-scatter.28
  2125.4 41.1 reduce-scatter.12
  2170.9 41.2 reduce-scatter.14
  2215.9 51.3 reduce-scatter.16
  2271.6 51.3 reduce-scatter.22
  2326.7 51.2 reduce-scatter.18
  2381.9 33.3 reduce-scatter.20
